TPU v7x, 256 devices: a whole 4x4x8 slice. The times are simulated.
256 devices in a mesh: leaf: 32 (over x, y, core), front: 8 (over z).
Axes of the slice: x: 4, y: 4, z: 8, core: 2. Of those that a mesh axis runs over, the one named last changes fastest.
Arguments:
- child_updates: float32 [32768, 1024], P('leaf', 'front'), as said below
- initial_one: float32 [32768, 2048], P('leaf', 'front'), as said below
- initial_two: float32 [16384, 2048], P('leaf', 'front'), as said below
- pattern_one: int32 [16, 16, 16], replicated, may hold values 0 or 1
- pattern_two: int32 [8, 16, 16], replicated, may hold values 0 or 1
- parent_map_one: int32 [16, 2, 16], replicated, may hold values from 0 to 15, each once within a row
- parent_map_two: int32 [8, 2, 16], replicated, may hold values from 0 to 15, each once within a row
Outputs:
- factor_one: float32 [32768, 1024], P('leaf', 'front')
- factor_two: float32 [16384, 1024], P('leaf', 'front')
- schur_two: float32 [8192, 1024], P('leaf', 'front')
Inputs may be any that keep to these rules, and one draw needn't show every extreme that they name: `parent_map_one`: each row is a permutation of 0 to 15; only its first 8 entries are used. `parent_map_two`: each row is a permutation of 0 to 15; only its first 8 entries are used. `initial_one`: each 2048 x 2048 front block is symmetric, and positive definite after any symmetric block mask. `initial_two`: each 2048 x 2048 front block is symmetric, and positive definite after any symmetric block mask. `child_updates`: each 1024 x 1024 matrix is symmetric positive definite.
All inputs are finite; a program needn't handle non-finite values.
Results may differ from a plain program's by a relative error of at most 0.0003.
Values sent between devices are 32-bit elements; how exact they have to be, the bound alone decides.
No kernel may reach another device: no remote copies, remote signals or barrier semaphores. Data moves between devices by JAX's collectives and lax.ppermute only.
A program may use at most 128 MiB of HBM per device.

v0:
```python
import jax
import jax.numpy as jnp
from jax import lax
from jax.sharding import PartitionSpec as P

BLK = 128
SEP = 1024
UPD = 1024
FR = 2048
HIGHEST = lax.Precision.HIGHEST


def swapped(block, axis, stride):
    count = lax.axis_size(axis)
    route = []
    for low in range(count):
        high = low | 1 << stride
        if high != low and high < count:
            route += [(low, high), (high, low)]
    return lax.ppermute(block, axis, route)


def spread(block, axis, holder):
    block = jnp.where(lax.axis_index(axis) == holder, block, jnp.zeros_like(block))
    return lax.psum(block, axis)


def solve_rows(chol_block, right_side):
    return jax.scipy.linalg.solve_triangular(chol_block, right_side.T, lower=True).T


def gather_subcube(pieces, level_depth, leaf_index):
    for bit_number in range(level_depth):
        partner = swapped(pieces, "leaf", bit_number)
        upper_half = leaf_index >> bit_number & 1 == 1
        pieces = jnp.where(
            upper_half, jnp.concatenate([partner, pieces], 0), jnp.concatenate([pieces, partner], 0)
        )
    return pieces


def fetch_rows(pieces, wanted, level_depth, leaf_index):
    columns = pieces.shape[1]
    full_panel = gather_subcube(pieces, level_depth, leaf_index)
    return jnp.take(full_panel.reshape(FR // BLK, BLK, columns), wanted, axis=0).reshape(
        wanted.shape[0] * BLK, columns
    )


def merge_halves(placed, level_depth, leaf_index):
    for bit_number in reversed(range(level_depth)):
        middle = placed.shape[0] // 2
        upper_half = leaf_index >> bit_number & 1 == 1
        kept_half = jnp.where(upper_half, placed[middle:], placed[:middle])
        given_half = jnp.where(upper_half, placed[:middle], placed[middle:])
        placed = kept_half + swapped(given_half, "leaf", bit_number)
    return placed


def assemble(
    child_tile, initial, pattern, parent_map, level_depth, leaf_index, front_index, col_blocks
):
    group_share = 2**level_depth
    child_share = group_share // 2
    front_group = leaf_index // group_share
    child_side = leaf_index // child_share % 2
    child_sub = leaf_index % child_share
    sub_index = leaf_index % group_share
    update_blocks = UPD // BLK
    front_blocks = FR // BLK
    tile_cols = 2 * col_blocks * BLK
    gathered = lax.all_gather(child_tile, "front", axis=1, tiled=True)
    child_rows = gathered.shape[0]
    child_row_blocks = child_rows // BLK
    both_maps = lax.dynamic_index_in_dim(parent_map, front_group, 0, keepdims=False)
    block_map = lax.dynamic_index_in_dim(both_maps, child_side, 0, keepdims=False)[:update_blocks]
    target_cols = 2 * col_blocks * front_index + jnp.arange(2 * col_blocks, dtype=jnp.int32)
    col_pick = (block_map[:, None] == target_cols[None, :]).astype(jnp.float32)
    picked = jnp.einsum(
        "rik,it->rtk", gathered.reshape(child_rows, update_blocks, BLK), col_pick, precision=HIGHEST
    )
    my_map = lax.dynamic_slice_in_dim(block_map, child_sub * child_row_blocks, child_row_blocks)
    row_place = (jnp.arange(front_blocks, dtype=jnp.int32)[:, None] == my_map[None, :]).astype(
        jnp.float32
    )
    placed = jnp.einsum(
        "ba,akc->bkc",
        row_place,
        picked.reshape(child_row_blocks, BLK, tile_cols),
        precision=HIGHEST,
    ).reshape(FR, tile_cols)
    merged = merge_halves(placed, level_depth, leaf_index)
    own_blocks = front_blocks // group_share
    whole_pattern = lax.dynamic_index_in_dim(pattern, front_group, 0, keepdims=False)
    row_part = lax.dynamic_slice_in_dim(whole_pattern, sub_index * own_blocks, own_blocks, 0)
    row_part = lax.dynamic_slice_in_dim(row_part, 2 * col_blocks * front_index, 2 * col_blocks, 1)
    col_part = lax.dynamic_slice_in_dim(
        whole_pattern, 2 * col_blocks * front_index, 2 * col_blocks, 0
    )
    col_part = lax.dynamic_slice_in_dim(col_part, sub_index * own_blocks, own_blocks, 1)
    row_ids = sub_index * own_blocks + jnp.arange(own_blocks, dtype=jnp.int32)
    keep_blocks = (row_part == 1) | (col_part.T == 1) | (row_ids[:, None] == target_cols[None, :])
    keep_mask = (
        jnp.broadcast_to(keep_blocks[:, None, :, None], (own_blocks, BLK, 2 * col_blocks, BLK))
        .reshape(own_blocks * BLK, tile_cols)
        .astype(jnp.float32)
    )
    return (initial * keep_mask + merged, row_ids, target_cols)


def factor_panels(
    front_tile, row_ids, target_cols, level_depth, leaf_index, front_index, col_blocks
):
    tile_rows = front_tile.shape[0]
    panel_width = col_blocks * BLK
    row_odd = jnp.repeat(row_ids % 2 == 1, BLK)
    row_sep = jnp.repeat(row_ids // 2, BLK)
    col_odd = jnp.repeat(target_cols % 2 == 1, BLK)
    col_sep = jnp.repeat(target_cols // 2, BLK)
    factor_tile = jnp.zeros((tile_rows, col_blocks, BLK), jnp.float32)
    for step_index in range(lax.axis_size("front")):
        first_block = step_index * col_blocks
        panel_slots = first_block + jnp.arange(col_blocks, dtype=jnp.int32)
        sep_cols = front_tile.reshape(tile_rows, 2 * col_blocks, BLK)[:, 0::2].reshape(
            tile_rows, panel_width
        )
        panel_rows = spread(sep_cols, "front", step_index)
        wanted = jnp.concatenate([2 * panel_slots, target_cols])
        fetched = fetch_rows(panel_rows, wanted, level_depth, leaf_index)
        chol_block = jnp.linalg.cholesky(fetched[:panel_width])
        own_factor = solve_rows(chol_block, panel_rows)
        col_factor = solve_rows(chol_block, fetched[panel_width:])
        own_keep = (row_odd | (row_sep >= first_block + col_blocks)).astype(jnp.float32)
        col_keep = (col_odd | (col_sep >= first_block + col_blocks)).astype(jnp.float32)
        front_tile = front_tile - jnp.dot(
            own_factor * own_keep[:, None], (col_factor * col_keep[:, None]).T, precision=HIGHEST
        )
        valid_rows = (row_odd[:, None] | (row_sep[:, None] >= panel_slots[None, :])).astype(
            jnp.float32
        )
        factor_tile = jnp.where(
            front_index == step_index,
            own_factor.reshape(tile_rows, col_blocks, BLK) * valid_rows[:, :, None],
            factor_tile,
        )
    schur_tile = front_tile.reshape(tile_rows // BLK, BLK, 2 * col_blocks, BLK)[
        1::2, :, 1::2, :
    ].reshape(tile_rows // 2, col_blocks * BLK)
    return (factor_tile.reshape(tile_rows, col_blocks * BLK), schur_tile)


def per_device(
    child_updates,
    initial_one,
    initial_two,
    pattern_one,
    pattern_two,
    parent_map_one,
    parent_map_two,
):
    leaf_index = lax.axis_index("leaf")
    front_index = lax.axis_index("front")
    col_blocks = SEP // BLK // lax.axis_size("front")
    child_tile = child_updates
    factors = []
    for level_depth, initial, pattern, parent_map in (
        (1, initial_one, pattern_one, parent_map_one),
        (2, initial_two, pattern_two, parent_map_two),
    ):
        front_tile, row_ids, target_cols = assemble(
            child_tile,
            initial,
            pattern,
            parent_map,
            level_depth,
            leaf_index,
            front_index,
            col_blocks,
        )
        factor_tile, child_tile = factor_panels(
            front_tile, row_ids, target_cols, level_depth, leaf_index, front_index, col_blocks
        )
        factors.append(factor_tile)
    return (factors[0], factors[1], child_tile)


def solution(mesh):
    placed = (P("leaf", "front"), P("leaf", "front"), P("leaf", "front"), P(), P(), P(), P())
    return jax.shard_map(
        per_device,
        mesh=mesh,
        in_specs=placed,
        out_specs=(P("leaf", "front"), P("leaf", "front"), P("leaf", "front")),
        check_vma=False,
    )
```

profile of v0, /device:TPU:1, one launch (start us, length us, event | category | flops | bytes accessed | tf_op | source)
XLA Modules:
  0.0 1970.0 jit_solution(7487446941033398264)
XLA Ops:
  8.1 65.2 %all-gather.3.cloned.1.call-done = f32[1024,1024]{1,0:T(8,128)} async-done(((f32[1024,128]{1,0:T(8,128)}), f32[1024,1024]{1,0:T(8,128)}) %all-gather.3.cloned.1.call-update) | async-done | bytes 4194320 | tf_op jit(solution)/shard_map/all_gather | solution.py:72
  96.0 64.8 %all-reduce.17.cloned.1.call-done = f32[1024,128]{0,1:T(8,128)} async-done(((f32[1024,128]{0,1:T(8,128)}), f32[1024,128]{0,1:T(8,128)}) %all-reduce.17.cloned.1.call-update) | async-done | bytes 524304 | tf_op jit(solution)/shard_map/psum | solution.py:25
  172.7 11.7 cholesky.254
  185.8 9.8 custom-call.40
  198.7 67.0 %all-reduce.19.cloned.1.call-done = f32[1024,128]{0,1:T(8,128)} async-done(((f32[1024,128]{0,1:T(8,128)}), f32[1024,128]{0,1:T(8,128)}) %all-reduce.19.cloned.1.call-update) | async-done | bytes 524304 | tf_op jit(solution)/shard_map/psum | solution.py:25
  277.9 11.7 cholesky.265
  291.0 9.8 custom-call.42
  303.9 67.0 %all-reduce.21.cloned.1.call-done = f32[1024,128]{0,1:T(8,128)} async-done(((f32[1024,128]{0,1:T(8,128)}), f32[1024,128]{0,1:T(8,128)}) %all-reduce.21.cloned.1.call-update) | async-done | bytes 524304 | tf_op jit(solution)/shard_map/psum | solution.py:25
  382.9 11.7 cholesky.276
  395.9 9.8 custom-call.44
  408.9 67.0 %all-reduce.23.cloned.1.call-done = f32[1024,128]{0,1:T(8,128)} async-done(((f32[1024,128]{0,1:T(8,128)}), f32[1024,128]{0,1:T(8,128)}) %all-reduce.23.cloned.1.call-update) | async-done | bytes 524304 | tf_op jit(solution)/shard_map/psum | solution.py:25
  488.0 11.7 cholesky.287
  501.1 9.8 custom-call.46
  513.9 67.0 %all-reduce.25.cloned.1.call-done = f32[1024,128]{0,1:T(8,128)} async-done(((f32[1024,128]{0,1:T(8,128)}), f32[1024,128]{0,1:T(8,128)}) %all-reduce.25.cloned.1.call-update) | async-done | bytes 524304 | tf_op jit(solution)/shard_map/psum | solution.py:25
  593.1 11.7 cholesky.298
  619.1 67.0 %all-reduce.27.cloned.1.call-done = f32[1024,128]{0,1:T(8,128)} async-done(((f32[1024,128]{0,1:T(8,128)}), f32[1024,128]{0,1:T(8,128)}) %all-reduce.27.cloned.1.call-update) | async-done | bytes 524304 | tf_op jit(solution)/shard_map/psum | solution.py:25
  698.4 11.7 cholesky.309
  724.3 67.1 %all-reduce.29.cloned.1.call-done = f32[1024,128]{0,1:T(8,128)} async-done(((f32[1024,128]{0,1:T(8,128)}), f32[1024,128]{0,1:T(8,128)}) %all-reduce.29.cloned.1.call-update) | async-done | bytes 524304 | tf_op jit(solution)/shard_map/psum | solution.py:25
  803.4 11.7 cholesky.320
  829.3 67.1 %all-reduce.31.cloned.1.call-done = f32[1024,128]{0,1:T(8,128)} async-done(((f32[1024,128]{0,1:T(8,128)}), f32[1024,128]{0,1:T(8,128)}) %all-reduce.31.cloned.1.call-update) | async-done | bytes 524304 | tf_op jit(solution)/shard_map/psum | solution.py:25
  908.4 11.7 cholesky.331
  936.3 40.7 %all-gather.5.cloned.1.call-done = f32[512,1024]{1,0:T(8,128)} async-done(((f32[512,128]{1,0:T(8,128)}), f32[512,1024]{1,0:T(8,128)}) %all-gather.5.cloned.1.call-update) | async-done | bytes 2097168 | tf_op jit(solution)/shard_map/all_gather | solution.py:72
  987.9 15.9 collective-permute-done.9
  1016.5 65.7 %all-reduce.33.cloned.1.call-done = f32[512,128]{0,1:T(8,128)} async-done(((f32[512,128]{0,1:T(8,128)}), f32[512,128]{0,1:T(8,128)}) %all-reduce.33.cloned.1.call-update) | async-done | bytes 262160 | tf_op jit(solution)/shard_map/psum | solution.py:25
  1091.7 11.8 collective-permute-done.12
  1107.2 11.7 cholesky.342
  1132.3 67.0 %all-reduce.35.cloned.1.call-done = f32[512,128]{0,1:T(8,128)} async-done(((f32[512,128]{0,1:T(8,128)}), f32[512,128]{0,1:T(8,128)}) %all-reduce.35.cloned.1.call-update) | async-done | bytes 262160 | tf_op jit(solution)/shard_map/psum | solution.py:25
  1208.6 11.8 collective-permute-done.14
  1224.1 11.7 cholesky.353
  1249.3 67.1 %all-reduce.37.cloned.1.call-done = f32[512,128]{0,1:T(8,128)} async-done(((f32[512,128]{0,1:T(8,128)}), f32[512,128]{0,1:T(8,128)}) %all-reduce.37.cloned.1.call-update) | async-done | bytes 262160 | tf_op jit(solution)/shard_map/psum | solution.py:25
  1325.7 11.8 collective-permute-done.16
  1341.2 11.7 cholesky.364
  1366.4 67.0 %all-reduce.39.cloned.1.call-done = f32[512,128]{0,1:T(8,128)} async-done(((f32[512,128]{0,1:T(8,128)}), f32[512,128]{0,1:T(8,128)}) %all-reduce.39.cloned.1.call-update) | async-done | bytes 262160 | tf_op jit(solution)/shard_map/psum | solution.py:25
  1442.7 11.8 collective-permute-done.18
  1458.2 11.7 cholesky.375
  1483.5 67.0 %all-reduce.41.cloned.1.call-done = f32[512,128]{0,1:T(8,128)} async-done(((f32[512,128]{0,1:T(8,128)}), f32[512,128]{0,1:T(8,128)}) %all-reduce.41.cloned.1.call-update) | async-done | bytes 262160 | tf_op jit(solution)/shard_map/psum | solution.py:25
  1560.0 11.8 collective-permute-done.20
  1575.5 11.7 cholesky.386
  1600.8 67.0 %all-reduce.43.cloned.1.call-done = f32[512,128]{0,1:T(8,128)} async-done(((f32[512,128]{0,1:T(8,128)}), f32[512,128]{0,1:T(8,128)}) %all-reduce.43.cloned.1.call-update) | async-done | bytes 262160 | tf_op jit(solution)/shard_map/psum | solution.py:25
  1677.0 11.8 collective-permute-done.22
  1692.5 11.7 cholesky.397
  1705.6 9.8 custom-call.66
  1718.5 67.0 %all-reduce.45.cloned.1.call-done = f32[512,128]{0,1:T(8,128)} async-done(((f32[512,128]{0,1:T(8,128)}), f32[512,128]{0,1:T(8,128)}) %all-reduce.45.cloned.1.call-update) | async-done | bytes 262160 | tf_op jit(solution)/shard_map/psum | solution.py:25
  1795.9 10.7 collective-permute-done.24
  1810.3 11.7 cholesky.408
  1823.4 10.4 custom-call.68
  1840.7 67.0 %all-reduce.47.cloned.1.call-done = f32[512,128]{0,1:T(8,128)} async-done(((f32[512,128]{0,1:T(8,128)}), f32[512,128]{0,1:T(8,128)}) %all-reduce.47.cloned.1.call-update) | async-done | bytes 262160 | tf_op jit(solution)/shard_map/psum | solution.py:25
  1935.3 11.7 cholesky.419
  (617 shorter events, 433.0 us)
Async XLA Ops:
  7.2 66.1 %all-gather.3.cloned.1.call-start = ((), (), s32[]{:S(2)}) async-start(), calls=%async_computation | async-start | bytes 4718592 | tf_op jit(solution)/shard_map/all_gather | solution.py:72
  7.9 152.8 %all-reduce.17.cloned.1.call-start = ((), (), s32[]{:S(2)}) async-start(), calls=%async_computation.1 | async-start | bytes 1048576 | tf_op jit(solution)/shard_map/psum | solution.py:25
  82.8 10.4 collective-permute-start
  95.8 169.9 %all-reduce.19.cloned.1.call-start = ((), (), s32[]{:S(2)}) async-start(), calls=%async_computation.2 | async-start | bytes 1048576 | tf_op jit(solution)/shard_map/psum | solution.py:25
  95.9 812.2 %copy-start.63 = (pred[3]{0:T(512)(128)(4,1)}, pred[3]{0:T(512)(128)(4,1)S(1)}, u32[]{:S(2)}) copy-start(pred[3]{0:T(512)(128)(4,1)S(1)} %get-tuple-element.14) | copy-start | bytes 13
  160.7 7.2 collective-permute-start.1
  198.6 172.3 %all-reduce.21.cloned.1.call-start = ((), (), s32[]{:S(2)}) async-start(), calls=%async_computation.3 | async-start | bytes 1048576 | tf_op jit(solution)/shard_map/psum | solution.py:25
  265.7 7.4 collective-permute-start.2
  303.8 172.1 %all-reduce.23.cloned.1.call-start = ((), (), s32[]{:S(2)}) async-start(), calls=%async_computation.4 | async-start | bytes 1048576 | tf_op jit(solution)/shard_map/psum | solution.py:25
  303.9 602.3 %copy-start.62 = (s32[1024]{0:T(1024)}, s32[1024]{0:T(1024)S(1)}, u32[]{:S(2)}) copy-start(s32[1024]{0:T(1024)S(1)} %get-tuple-element.48) | copy-start | bytes 12292
  370.9 7.1 collective-permute-start.3
  408.7 172.2 %all-reduce.25.cloned.1.call-start = ((), (), s32[]{:S(2)}) async-start(), calls=%async_computation.5 | async-start | bytes 1048576 | tf_op jit(solution)/shard_map/psum | solution.py:25
  475.9 7.2 collective-permute-start.4
  513.9 172.2 %all-reduce.27.cloned.1.call-start = ((), (), s32[]{:S(2)}) async-start(), calls=%async_computation.6 | async-start | bytes 1048576 | tf_op jit(solution)/shard_map/psum | solution.py:25
  581.0 7.2 collective-permute-start.5
  619.0 172.4 %all-reduce.29.cloned.1.call-start = ((), (), s32[]{:S(2)}) async-start(), calls=%async_computation.7 | async-start | bytes 1048576 | tf_op jit(solution)/shard_map/psum | solution.py:25
  686.1 7.4 collective-permute-start.6
  724.2 172.1 %all-reduce.31.cloned.1.call-start = ((), (), s32[]{:S(2)}) async-start(), calls=%async_computation.8 | async-start | bytes 1048576 | tf_op jit(solution)/shard_map/psum | solution.py:25
  791.4 7.1 collective-permute-start.7
  829.2 147.8 %all-gather.5.cloned.1.call-start = ((), (), s32[]{:S(2)}) async-start(), calls=%async_computation.9 | async-start | bytes 2359296 | tf_op jit(solution)/shard_map/all_gather | solution.py:72
  896.4 7.2 collective-permute-start.8
  935.2 147.0 %all-reduce.33.cloned.1.call-start = ((), (), s32[]{:S(2)}) async-start(), calls=%async_computation.10 | async-start | bytes 524288 | tf_op jit(solution)/shard_map/psum | solution.py:25
  983.8 20.0 %collective-permute-start.9 = (f32[1024,256]{0,1:T(8,128)}, f32[1024,256]{0,1:T(8,128)}, u32[]{:S(2)}, u32[]{:S(2)}) collective-permute-start(f32[1024,256]{0,1:T(8,128)} %copy.86), channel_id=1, source_target_pairs={{0,16},{16,0},{8,24},{24,8},{32,48},{48,32},{40,56},{56,40},{64,80... | collective-permute-start | bytes 3145736 | tf_op jit(solution)/shard_map/ppermute | solution.py:20
  1005.3 9.0 collective-permute-start.10
  1016.5 182.9 %all-reduce.35.cloned.1.call-start = ((), (), s32[]{:S(2)}) async-start(), calls=%async_computation.11 | async-start | bytes 524288 | tf_op jit(solution)/shard_map/psum | solution.py:25
  1082.2 6.6 collective-permute-start.11
  1089.8 13.7 collective-permute-start.12
  1132.3 184.1 %all-reduce.37.cloned.1.call-start = ((), (), s32[]{:S(2)}) async-start(), calls=%async_computation.12 | async-start | bytes 524288 | tf_op jit(solution)/shard_map/psum | solution.py:25
  1199.4 6.6 collective-permute-start.13
  1207.0 13.4 collective-permute-start.14
  1249.3 184.1 %all-reduce.39.cloned.1.call-start = ((), (), s32[]{:S(2)}) async-start(), calls=%async_computation.13 | async-start | bytes 524288 | tf_op jit(solution)/shard_map/psum | solution.py:25
  1316.4 6.6 collective-permute-start.15
  1324.1 13.4 collective-permute-start.16
  1366.4 184.1 %all-reduce.41.cloned.1.call-start = ((), (), s32[]{:S(2)}) async-start(), calls=%async_computation.14 | async-start | bytes 524288 | tf_op jit(solution)/shard_map/psum | solution.py:25
  1433.4 6.6 collective-permute-start.17
  1441.1 13.5 collective-permute-start.18
  1483.4 184.4 %all-reduce.43.cloned.1.call-start = ((), (), s32[]{:S(2)}) async-start(), calls=%async_computation.15 | async-start | bytes 524288 | tf_op jit(solution)/shard_map/psum | solution.py:25
  1550.5 6.6 collective-permute-start.19
  1558.2 13.7 collective-permute-start.20
  1600.7 184.8 %all-reduce.45.cloned.1.call-start = ((), (), s32[]{:S(2)}) async-start(), calls=%async_computation.16 | async-start | bytes 524288 | tf_op jit(solution)/shard_map/psum | solution.py:25
  1667.8 6.6 collective-permute-start.21
  1675.5 13.4 collective-permute-start.22
  1716.2 90.6 %copy-start.23 = (f32[128,512]{1,0:T(8,128)}, f32[128,512]{1,0:T(8,128)S(1)}, u32[]{:S(2)}) copy-start(f32[128,512]{1,0:T(8,128)S(1)} %fusion.49) | copy-start | bytes 786436
  1718.4 189.3 %all-reduce.47.cloned.1.call-start = ((), (), s32[]{:S(2)}) async-start(), calls=%async_computation.17 | async-start | bytes 524288 | tf_op jit(solution)/shard_map/psum | solution.py:25
  1785.5 6.6 collective-permute-start.23
  1793.2 13.4 collective-permute-start.24
  1907.7 6.6 collective-permute-start.25
  1916.1 13.7 collective-permute-start.26
  (65 other events, 1790.7 us)
Sparse Core Ops, SparseCore 0:
  9.7 63.4 all-gather.2
  95.9 64.7 all-reduce.16
  198.7 66.9 all-reduce.18
  303.9 66.9 all-reduce.20
  408.9 67.0 all-reduce.22
  514.0 66.9 all-reduce.24
  619.1 66.9 all-reduce.26
  724.3 66.9 all-reduce.28
  829.3 66.9 all-reduce.30
  935.3 41.6 all-gather.4
  1016.6 65.5 all-reduce.32
  1132.4 66.9 all-reduce.34
  1249.4 66.9 all-reduce.36
  1366.5 66.9 all-reduce.38
  1483.5 66.9 all-reduce.40
  1600.8 66.9 all-reduce.42
  1718.6 66.9 all-reduce.44
  1840.7 66.9 all-reduce.46
where the time goes:
time: 1980 us; the launch traced here: 1970 us
  waiting for transfers between devices  1300 us (66%)
  other arithmetic  415 us (21%)
  starting transfers between devices  111 us (6%)
  local copies, waits for them, and re-layouts  86 us (4%)
  matrix products  35.7 us (2%)
    psum x16, waiting for transfers between devices, spread(): return lax.psum(block, axis)  1070 us
    another operation x48, other arithmetic, factor_panels(): chol_block = jnp.linalg.cholesky(fetched[:panel_width])  198 us
    another operation x32, other arithmetic, solve_rows(): jax.scipy.linalg.solve_triangular(chol_block, right_side.T, lower=True)  168 us
    ppermute x27, waiting for transfers between devices, swapped(): return lax.ppermute(block, axis, route)  128 us
    ppermute x27, starting transfers between devices, swapped(): return lax.ppermute(block, axis, route)  110 us
    all_gather x2, waiting for transfers between devices, assemble(): gathered = lax.all_gather(child_tile, 'front', axis=1, tiled=True)  106 us
  transfers between devices with their start and end apart: 45, of which 43 were waited for; matrix products, arithmetic and copies ran while one was open for 1% of the time, Pallas kernels for 0%

commit v1 on v0

--- a/solution.py
+++ b/solution.py
@@ -22,7 +22,7 @@
 
 def spread(block, axis, holder):
     block = jnp.where(lax.axis_index(axis) == holder, block, jnp.zeros_like(block))
-    return lax.psum(block, axis)
+    return jnp.sum(lax.all_gather(block, axis), axis=0)
 
 
 def solve_rows(chol_block, right_side):

time: 1980 us -> 1650 us (0.83)
  waiting for transfers between devices: 1300 us -> 946 us
  local copies, waits for them, and re-layouts: 86 us -> 164 us
  starting transfers between devices: 111 us -> 72.4 us
    psum x16 -> x0, waiting for transfers between devices: 1070 us -> none  [spread(): return lax.psum(block, axis)]
    all_gather x0 -> x16, waiting for transfers between devices: none -> 713 us  [spread(): return jnp.sum(lax.all_gather(block, axis), axis=0)]
    unnamed x143 -> x113, local copies, waits for them, and re-layouts: 12.7 us -> 81.6 us
    ppermute x27, starting transfers between devices: 110 us -> 69.4 us  [swapped(): return lax.ppermute(block, axis, route)]
where the time goes in v1:
time: 1650 us
  waiting for transfers between devices  946 us (57%)
  other arithmetic  413 us (25%)
  local copies, waits for them, and re-layouts  164 us (10%)
  starting transfers between devices  72.4 us (4%)
  matrix products  33.4 us (2%)
  between operations  17.5 us (1%)
    all_gather x16, waiting for transfers between devices, spread(): return jnp.sum(lax.all_gather(block, axis), axis=0)  713 us
    another operation x48, other arithmetic, factor_panels(): chol_block = jnp.linalg.cholesky(fetched[:panel_width])  198 us
    another operation x32, other arithmetic, solve_rows(): jax.scipy.linalg.solve_triangular(chol_block, right_side.T, lower=True)  167 us
    ppermute x27, waiting for transfers between devices, swapped(): return lax.ppermute(block, axis, route)  127 us
    all_gather x2, waiting for transfers between devices, assemble(): gathered = lax.all_gather(child_tile, 'front', axis=1, tiled=True)  106 us
    unnamed x113, local copies, waits for them, and re-layouts  81.6 us
    ppermute x27, starting transfers between devices, swapped(): return lax.ppermute(block, axis, route)  69.4 us
  transfers between devices with their start and end apart: 45, of which 43 were waited for; matrix products, arithmetic and copies ran while one was open for 1% of the time, Pallas kernels for 0%

profile of v1, /device:TPU:1, one launch (start us, length us, event | category | flops | bytes accessed | tf_op | source)
XLA Modules:
  0.0 1646.5 jit_solution(13409655176662429897)
XLA Ops:
  8.1 65.2 %all-gather.35.cloned.1.call-done = f32[1024,1024]{1,0:T(8,128)} async-done(((f32[1024,128]{1,0:T(8,128)}), f32[1024,1024]{1,0:T(8,128)}) %all-gather.35.cloned.1.call-update) | async-done | bytes 4194320 | tf_op jit(solution)/shard_map/all_gather | solution.py:72
  96.3 50.5 %all-gather.39.cloned.1.call-done = f32[8192,1,128]{0,2,1:T(8,128)} async-done(((f32[1024,1,128]{0,2,1:T(8,128)}), f32[8192,1,128]{0,2,1:T(8,128)}) %all-gather.39.cloned.1.call-update) | async-done | bytes 4194320 | tf_op jit(solution)/shard_map/all_gather | solution.py:25
  159.7 11.7 cholesky.254
  172.7 9.8 custom-call.40
  185.7 53.0 %all-gather.41.cloned.1.call-done = f32[8192,1,128]{0,2,1:T(8,128)} async-done(((f32[1024,1,128]{0,2,1:T(8,128)}), f32[8192,1,128]{0,2,1:T(8,128)}) %all-gather.41.cloned.1.call-update) | async-done | bytes 4194320 | tf_op jit(solution)/shard_map/all_gather | solution.py:25
  251.4 11.7 cholesky.265
  277.6 52.9 %all-gather.43.cloned.1.call-done = f32[8192,1,128]{0,2,1:T(8,128)} async-done(((f32[1024,1,128]{0,2,1:T(8,128)}), f32[8192,1,128]{0,2,1:T(8,128)}) %all-gather.43.cloned.1.call-update) | async-done | bytes 4194320 | tf_op jit(solution)/shard_map/all_gather | solution.py:25
  343.2 11.7 cholesky.276
  369.8 52.6 %all-gather.45.cloned.1.call-done = f32[8192,1,128]{0,2,1:T(8,128)} async-done(((f32[1024,1,128]{0,2,1:T(8,128)}), f32[8192,1,128]{0,2,1:T(8,128)}) %all-gather.45.cloned.1.call-update) | async-done | bytes 4194320 | tf_op jit(solution)/shard_map/all_gather | solution.py:25
  437.2 11.7 cholesky.287
  463.3 53.0 %all-gather.47.cloned.1.call-done = f32[8192,1,128]{0,2,1:T(8,128)} async-done(((f32[1024,1,128]{0,2,1:T(8,128)}), f32[8192,1,128]{0,2,1:T(8,128)}) %all-gather.47.cloned.1.call-update) | async-done | bytes 4194320 | tf_op jit(solution)/shard_map/all_gather | solution.py:25
  531.2 11.7 cholesky.298
  544.3 9.8 custom-call.48
  557.4 52.9 %all-gather.49.cloned.1.call-done = f32[8192,1,128]{0,2,1:T(8,128)} async-done(((f32[1024,1,128]{0,2,1:T(8,128)}), f32[8192,1,128]{0,2,1:T(8,128)}) %all-gather.49.cloned.1.call-update) | async-done | bytes 4194320 | tf_op jit(solution)/shard_map/all_gather | solution.py:25
  625.5 11.7 cholesky.309
  638.6 9.8 custom-call.50
  651.6 53.1 %all-gather.51.cloned.1.call-done = f32[8192,1,128]{0,2,1:T(8,128)} async-done(((f32[1024,1,128]{0,2,1:T(8,128)}), f32[8192,1,128]{0,2,1:T(8,128)}) %all-gather.51.cloned.1.call-update) | async-done | bytes 4194320 | tf_op jit(solution)/shard_map/all_gather | solution.py:25
  719.5 11.7 cholesky.320
  732.6 9.8 custom-call.52
  745.7 53.0 %all-gather.53.cloned.1.call-done = f32[8192,1,128]{0,2,1:T(8,128)} async-done(((f32[1024,1,128]{0,2,1:T(8,128)}), f32[8192,1,128]{0,2,1:T(8,128)}) %all-gather.53.cloned.1.call-update) | async-done | bytes 4194320 | tf_op jit(solution)/shard_map/all_gather | solution.py:25
  813.7 11.7 cholesky.331
  841.5 40.9 %all-gather.37.cloned.1.call-done = f32[512,1024]{1,0:T(8,128)} async-done(((f32[512,128]{1,0:T(8,128)}), f32[512,1024]{1,0:T(8,128)}) %all-gather.37.cloned.1.call-update) | async-done | bytes 2097168 | tf_op jit(solution)/shard_map/all_gather | solution.py:72
  896.6 14.9 collective-permute-done.9
  925.2 35.1 %all-gather.55.cloned.1.call-done = f32[4096,1,128]{0,2,1:T(8,128)} async-done(((f32[512,1,128]{0,2,1:T(8,128)}), f32[4096,1,128]{0,2,1:T(8,128)}) %all-gather.55.cloned.1.call-update) | async-done | bytes 2097168 | tf_op jit(solution)/shard_map/all_gather | solution.py:25
  971.4 11.8 collective-permute-done.12
  987.0 11.7 cholesky.342
  1012.1 36.6 %all-gather.57.cloned.1.call-done = f32[4096,1,128]{0,2,1:T(8,128)} async-done(((f32[512,1,128]{0,2,1:T(8,128)}), f32[4096,1,128]{0,2,1:T(8,128)}) %all-gather.57.cloned.1.call-update) | async-done | bytes 2097168 | tf_op jit(solution)/shard_map/all_gather | solution.py:25
  1059.9 11.8 collective-permute-done.14
  1075.5 11.7 cholesky.353
  1088.6 9.8 custom-call.58
  1101.5 36.6 %all-gather.59.cloned.1.call-done = f32[4096,1,128]{0,2,1:T(8,128)} async-done(((f32[512,1,128]{0,2,1:T(8,128)}), f32[4096,1,128]{0,2,1:T(8,128)}) %all-gather.59.cloned.1.call-update) | async-done | bytes 2097168 | tf_op jit(solution)/shard_map/all_gather | solution.py:25
  1149.1 11.8 collective-permute-done.16
  1164.7 11.7 cholesky.364
  1189.9 36.6 %all-gather.61.cloned.1.call-done = f32[4096,1,128]{0,2,1:T(8,128)} async-done(((f32[512,1,128]{0,2,1:T(8,128)}), f32[4096,1,128]{0,2,1:T(8,128)}) %all-gather.61.cloned.1.call-update) | async-done | bytes 2097168 | tf_op jit(solution)/shard_map/all_gather | solution.py:25
  1237.6 11.8 collective-permute-done.18
  1253.1 11.7 cholesky.375
  1279.1 36.6 %all-gather.63.cloned.1.call-done = f32[4096,1,128]{0,2,1:T(8,128)} async-done(((f32[512,1,128]{0,2,1:T(8,128)}), f32[4096,1,128]{0,2,1:T(8,128)}) %all-gather.63.cloned.1.call-update) | async-done | bytes 2097168 | tf_op jit(solution)/shard_map/all_gather | solution.py:25
  1326.8 11.9 collective-permute-done.20
  1342.5 11.7 cholesky.386
  1367.7 36.6 %all-gather.65.cloned.1.call-done = f32[4096,1,128]{0,2,1:T(8,128)} async-done(((f32[512,1,128]{0,2,1:T(8,128)}), f32[4096,1,128]{0,2,1:T(8,128)}) %all-gather.65.cloned.1.call-update) | async-done | bytes 2097168 | tf_op jit(solution)/shard_map/all_gather | solution.py:25
  1415.3 11.8 collective-permute-done.22
  1430.8 11.7 cholesky.397
  1443.9 9.8 custom-call.66
  1456.8 36.6 %all-gather.67.cloned.1.call-done = f32[4096,1,128]{0,2,1:T(8,128)} async-done(((f32[512,1,128]{0,2,1:T(8,128)}), f32[4096,1,128]{0,2,1:T(8,128)}) %all-gather.67.cloned.1.call-update) | async-done | bytes 2097168 | tf_op jit(solution)/shard_map/all_gather | solution.py:25
  1504.5 11.8 collective-permute-done.24
  1520.0 11.7 cholesky.408
  1545.2 36.7 %all-gather.69.cloned.1.call-done = f32[4096,1,128]{0,2,1:T(8,128)} async-done(((f32[512,1,128]{0,2,1:T(8,128)}), f32[4096,1,128]{0,2,1:T(8,128)}) %all-gather.69.cloned.1.call-update) | async-done | bytes 2097168 | tf_op jit(solution)/shard_map/all_gather | solution.py:25
  1610.1 11.7 cholesky.419
  (595 shorter events, 466.2 us)
Async XLA Ops:
  7.2 66.1 %all-gather.35.cloned.1.call-start = ((), (), s32[]{:S(2)}) async-start(), calls=%async_computation | async-start | bytes 4718592 | tf_op jit(solution)/shard_map/all_gather | solution.py:72
  7.9 138.8 %all-gather.39.cloned.1.call-start = ((), (), s32[]{:S(2)}) async-start(), calls=%async_computation.2 | async-start | bytes 4718592 | tf_op jit(solution)/shard_map/all_gather | solution.py:25
  82.8 10.4 collective-permute-start
  95.8 143.0 %all-gather.41.cloned.1.call-start = ((), (), s32[]{:S(2)}) async-start(), calls=%async_computation.3 | async-start | bytes 4718592 | tf_op jit(solution)/shard_map/all_gather | solution.py:25
  153.2 2.8 collective-permute-start.1
  185.5 145.0 %all-gather.43.cloned.1.call-start = ((), (), s32[]{:S(2)}) async-start(), calls=%async_computation.4 | async-start | bytes 4718592 | tf_op jit(solution)/shard_map/all_gather | solution.py:25
  245.2 2.5 collective-permute-start.2
  277.3 145.1 %all-gather.45.cloned.1.call-start = ((), (), s32[]{:S(2)}) async-start(), calls=%async_computation.5 | async-start | bytes 4718592 | tf_op jit(solution)/shard_map/all_gather | solution.py:25
  337.0 2.6 collective-permute-start.3
  369.1 147.2 %all-gather.47.cloned.1.call-start = ((), (), s32[]{:S(2)}) async-start(), calls=%async_computation.6 | async-start | bytes 4718592 | tf_op jit(solution)/shard_map/all_gather | solution.py:25
  428.8 2.5 collective-permute-start.4
  463.0 147.3 %all-gather.49.cloned.1.call-start = ((), (), s32[]{:S(2)}) async-start(), calls=%async_computation.7 | async-start | bytes 4718592 | tf_op jit(solution)/shard_map/all_gather | solution.py:25
  522.8 2.6 collective-permute-start.5
  557.1 147.6 %all-gather.51.cloned.1.call-start = ((), (), s32[]{:S(2)}) async-start(), calls=%async_computation.8 | async-start | bytes 4718592 | tf_op jit(solution)/shard_map/all_gather | solution.py:25
  616.8 2.8 collective-permute-start.6
  651.4 147.3 %all-gather.53.cloned.1.call-start = ((), (), s32[]{:S(2)}) async-start(), calls=%async_computation.9 | async-start | bytes 4718592 | tf_op jit(solution)/shard_map/all_gather | solution.py:25
  711.1 2.5 collective-permute-start.7
  745.4 137.1 %all-gather.37.cloned.1.call-start = ((), (), s32[]{:S(2)}) async-start(), calls=%async_computation.1 | async-start | bytes 2359296 | tf_op jit(solution)/shard_map/all_gather | solution.py:72
  805.1 2.8 collective-permute-start.8
  840.5 119.9 %all-gather.55.cloned.1.call-start = ((), (), s32[]{:S(2)}) async-start(), calls=%async_computation.10 | async-start | bytes 2359296 | tf_op jit(solution)/shard_map/all_gather | solution.py:25
  891.5 20.0 %collective-permute-start.9 = (f32[1024,256]{0,1:T(8,128)}, f32[1024,256]{0,1:T(8,128)}, u32[]{:S(2)}, u32[]{:S(2)}) collective-permute-start(f32[1024,256]{0,1:T(8,128)} %copy.155), channel_id=1, source_target_pairs={{0,16},{16,0},{8,24},{24,8},{32,48},{48,32},{40,56},{56,40},{64,80... | collective-permute-start | bytes 3145736 | tf_op jit(solution)/shard_map/ppermute | solution.py:20
  914.1 8.7 collective-permute-start.10
  925.2 123.6 %all-gather.57.cloned.1.call-start = ((), (), s32[]{:S(2)}) async-start(), calls=%async_computation.11 | async-start | bytes 2359296 | tf_op jit(solution)/shard_map/all_gather | solution.py:25
  964.1 5.6 collective-permute-start.11
  969.8 13.4 collective-permute-start.12
  1012.1 126.0 %all-gather.59.cloned.1.call-start = ((), (), s32[]{:S(2)}) async-start(), calls=%async_computation.12 | async-start | bytes 2359296 | tf_op jit(solution)/shard_map/all_gather | solution.py:25
  1052.5 5.6 collective-permute-start.13
  1058.2 13.6 collective-permute-start.14
  1101.4 125.0 %all-gather.61.cloned.1.call-start = ((), (), s32[]{:S(2)}) async-start(), calls=%async_computation.13 | async-start | bytes 2359296 | tf_op jit(solution)/shard_map/all_gather | solution.py:25
  1141.9 5.6 collective-permute-start.15
  1147.5 13.4 collective-permute-start.16
  1188.1 41.7 %copy-start.22 = (f32[128,512]{1,0:T(8,128)}, f32[128,512]{1,0:T(8,128)S(1)}, u32[]{:S(2)}) copy-start(f32[128,512]{1,0:T(8,128)S(1)} %fusion.39) | copy-start | bytes 786436
  1189.8 125.9 %all-gather.63.cloned.1.call-start = ((), (), s32[]{:S(2)}) async-start(), calls=%async_computation.14 | async-start | bytes 2359296 | tf_op jit(solution)/shard_map/all_gather | solution.py:25
  1230.3 5.6 collective-permute-start.17
  1235.9 13.4 collective-permute-start.18
  1279.0 125.3 %all-gather.65.cloned.1.call-start = ((), (), s32[]{:S(2)}) async-start(), calls=%async_computation.15 | async-start | bytes 2359296 | tf_op jit(solution)/shard_map/all_gather | solution.py:25
  1319.5 5.6 collective-permute-start.19
  1325.1 13.6 collective-permute-start.20
  1365.9 41.6 %copy-start.26 = (f32[128,512]{1,0:T(8,128)}, f32[128,512]{1,0:T(8,128)S(1)}, u32[]{:S(2)}) copy-start(f32[128,512]{1,0:T(8,128)S(1)} %fusion.35) | copy-start | bytes 786436
  1367.6 125.8 %all-gather.67.cloned.1.call-start = ((), (), s32[]{:S(2)}) async-start(), calls=%async_computation.16 | async-start | bytes 2359296 | tf_op jit(solution)/shard_map/all_gather | solution.py:25
  1408.1 5.6 collective-permute-start.21
  1413.7 13.4 collective-permute-start.22
  1456.8 125.1 %all-gather.69.cloned.1.call-start = ((), (), s32[]{:S(2)}) async-start(), calls=%async_computation.17 | async-start | bytes 2359296 | tf_op jit(solution)/shard_map/all_gather | solution.py:25
  1497.2 5.6 collective-permute-start.23
  1502.9 13.4 collective-permute-start.24
  1543.4 41.6 %copy-start.30 = (f32[128,512]{1,0:T(8,128)}, f32[128,512]{1,0:T(8,128)S(1)}, u32[]{:S(2)}) copy-start(f32[128,512]{1,0:T(8,128)S(1)} %fusion.31) | copy-start | bytes 786436
  1585.7 5.6 collective-permute-start.25
  1591.3 13.6 collective-permute-start.26
  (42 other events, 435.6 us)
Sparse Core Ops, SparseCore 0:
  9.7 63.5 all-gather.34
  95.9 50.7 all-gather.38
  185.6 53.1 all-gather.40
  277.4 53.1 all-gather.42
  369.2 53.1 all-gather.44
  463.1 53.1 all-gather.46
  557.2 53.1 all-gather.48
  651.5 53.1 all-gather.50
  745.5 53.1 all-gather.52
  840.6 41.8 all-gather.36
  925.3 34.9 all-gather.54
  1012.2 36.5 all-gather.56
  1101.6 36.5 all-gather.58
  1189.9 36.5 all-gather.60
  1279.1 36.5 all-gather.62
  1367.7 36.5 all-gather.64
  1456.9 36.5 all-gather.66
  1545.3 36.5 all-gather.68
